TPU v7x, 32 devices: a whole 2x2x4 slice. The times are simulated.
32 devices in a mesh: band: 4 (over z), lev: 4 (over y, core), grp: 2 (over x).
Axes of the slice: x: 2, y: 2, z: 4, core: 2. Of those that a mesh axis runs over, the one named last changes fastest.
Arguments:
- fourier: bfloat16 [3, 8, 2, 2, 2, 48, 96], P(None, 'lev', None, None, 'grp', 'band'), may hold values from -6 to 6
- legendre: bfloat16 [96, 2, 48, 2, 48], P('band', None, 'lev', 'grp'), may hold values from -0.625 to 0.625
- lat_points: int32 [2, 48], P('grp', 'band'), may hold values from 20 to 400, as said below
- wave_slots: int32 [96], replicated, may hold values from 0 to 95, as said below
- vertical: float32 [8, 8], replicated, may hold values from -2 to 2
Outputs:
- spectral: bfloat16 [96, 2, 4, 8, 2, 48], P('band', None, None, None, None, ('lev', 'grp'))
Inputs may be any that keep to these rules, and one draw needn't show every extreme that they name: `lat_points`: the values are 20 + 4 i for i = 0 .. 95, each once (octahedral point counts of the latitude pairs, spread over devices). `wave_slots`: every wavenumber appears once; slots 2 i and 2 i + 1 hold wavenumbers m and 95 - m.
All inputs are finite; a program needn't handle non-finite values.
Results may differ from a plain program's by a relative error of at most 0.0053.
Values may be sent and summed in bfloat16 or wider, within the bound.
No kernel may reach another device: no remote copies, remote signals or barrier semaphores. Data moves between devices by JAX's collectives and lax.ppermute only.
A program may use at most 64 MiB of HBM per device.

v0:
```python
import jax
import jax.numpy as jnp
from jax import lax
from jax.sharding import PartitionSpec as P


def body(fourier, legendre, lat_points, wave_slots, vertical):
    wave_count = fourier.shape[6]
    cutoff = jnp.minimum(wave_count - 1, (lat_points - 1) // 2)
    wave_ids = lax.broadcasted_iota(jnp.int32, (1, 1, wave_count), 2)
    kept_mask = wave_ids <= cutoff[:, :, None]
    masked = jnp.where(kept_mask, fourier, jnp.zeros((), fourier.dtype))
    slot_table = (
        wave_slots[:, None] == lax.broadcasted_iota(jnp.int32, (wave_count, wave_count), 1)
    ).astype(jnp.bfloat16)
    ordered = lax.dot_general(
        slot_table, masked, (((1,), (6,)), ((), ())), preferred_element_type=jnp.float32
    ).astype(jnp.bfloat16)
    at_owners = lax.all_to_all(ordered, "band", split_axis=0, concat_axis=6, tiled=True)
    coeffs = lax.all_gather(at_owners, "lev", axis=2, tiled=True)
    level_count = coeffs.shape[2]
    level_rows = lax.broadcasted_iota(jnp.int32, (level_count, level_count), 0)
    level_cols = lax.broadcasted_iota(jnp.int32, (level_count, level_count), 1)
    integral = jnp.where(level_cols >= level_rows, vertical, jnp.zeros((), vertical.dtype))
    geopotential = jnp.einsum(
        "lk,skchgr->slchgr",
        integral,
        coeffs[:, 2].astype(jnp.float32),
        precision=lax.Precision.HIGHEST,
    ).astype(jnp.bfloat16)
    fields = jnp.concatenate([coeffs, geopotential[:, None]], axis=1)
    northern = fields[:, :, :, :, 0].astype(jnp.float32)
    southern = fields[:, :, :, :, 1].astype(jnp.float32)
    parity = jnp.stack(
        [(northern + southern).astype(jnp.bfloat16), (northern - southern).astype(jnp.bfloat16)],
        axis=4,
    )
    partial_value = lax.dot_general(
        parity, legendre, (((5, 6), (3, 4)), ((0, 4), (0, 1))), preferred_element_type=jnp.float32
    )
    summed = lax.psum_scatter(partial_value, "grp", scatter_dimension=5, tiled=True)
    slot_count = summed.shape[0]
    half_count = summed.shape[5]
    slot_waves = lax.dynamic_slice_in_dim(
        wave_slots, lax.axis_index("band") * slot_count, slot_count
    )
    block_start = (
        lax.axis_index("lev") * lax.axis_size("grp") + lax.axis_index("grp")
    ) * half_count
    half_ids = block_start + lax.broadcasted_iota(jnp.int32, (1, 1, half_count), 2)
    parity_ids = lax.broadcasted_iota(jnp.int32, (1, 2, 1), 1)
    total = slot_waves[:, None, None] + 2 * half_ids + parity_ids
    valid = (total <= wave_count - 1)[:, :, None, None, None, :]
    return jnp.where(valid, summed, 0.0).astype(jnp.bfloat16)


def solution(mesh):
    placed = (
        P(None, "lev", None, None, "grp", "band", None),
        P("band", None, "lev", "grp", None),
        P("grp", "band"),
        P(),
        P(),
    )
    return jax.shard_map(
        body,
        mesh=mesh,
        in_specs=placed,
        out_specs=P("band", None, None, None, None, ("lev", "grp")),
        check_vma=False,
    )
```

profile of v0, /device:TPU:0, one launch (start us, length us, event | category | flops | bytes accessed | tf_op | source)
XLA Modules:
  0.0 61.3 jit_solution(10844568631659761171)
XLA Ops:
  6.5 0.0 copy-start
  6.5 0.0 copy-start.2
  6.5 0.7 %minimum_bitcast_fusion = s32[12]{0:T(128)S(1)} fusion(s32[1,12]{1,0:T(1,128)} %param.7), kind=kLoop, calls=%fused_computation.34 | loop fusion | flops 204 | bytes 96 | tf_op jit(solution)/shard_map/le | solution.py:11
  7.3 0.1 iota_compare_fusion.1
  7.3 1.0 %fusion.9 = bf16[3,2,2,2,12,96]{5,3,4,2,1,0:T(2,128)(2,1)S(1)} fusion(bf16[3,2,2,2,1,12,96]{6,3,5,4,2,1,0:T(2,128)(2,1)} %param.5, pred[12,96]{1,0:T(8,128)(4,1)S(1)} %iota_compare_fusion.1), kind=kLoop, calls=%fused_computation.19 | loop fusion | flops 27648 | bytes 111744 | tf_op jit(solution)/shard_map/reshape.5
  8.3 0.9 %fusion.1 = bf16[96,3,2,2,2,1,12]{0,6,4,3,2,1,5:T(8,128)(2,1)S(1)} fusion(bf16[3,2,2,2,12,96]{5,3,4,2,1,0:T(2,128)(2,1)S(1)} %fusion.9, s32[96]{0:T(128)} %param.8), kind=kOutput, calls=%fused_computation.3 | convolution fusion | flops 5345280 | bytes 110976 | tf_op jit(solution)/shard_map/dot_general | solution.py:16
  9.2 0.7 %copy.19 = bf16[96,3,2,2,2,1,12]{6,4,3,2,1,5,0:T(2,128)(2,1)S(1)} copy(bf16[96,3,2,2,2,1,12]{0,6,4,3,2,1,5:T(8,128)(2,1)S(1)} %fusion.1) | data formatting | bytes 110592 | tf_op jit(solution)/shard_map/convert_element_type | solution.py:18
  9.8 1.7 %reshape.95 = bf16[4,2,3456]{2,1,0:T(2,128)(2,1)} reshape(bf16[96,1,3,2,2,2,12]{6,5,4,3,2,1,0:T(2,128)(2,1)S(1)} %bitcast.37) | data formatting | bytes 110592
  11.5 6.3 %all-to-all-start = ((bf16[4,2,3456]{2,1,0:T(2,128)(2,1)}), bf16[4,2,3456]{2,1,0:T(2,128)(2,1)S(1)}, u32[]{:S(2)}, u32[]{:S(2)}) async-start(bf16[4,2,3456]{2,1,0:T(2,128)(2,1)} %reshape.95), calls=%async_computation | async-start | bytes 110592 | tf_op jit(solution)/shard_map/all_to_all | solution.py:19
  17.9 0.0 reduce-scatter.2.cloned.1.call-start
  17.9 0.0 copy-done.2
  17.9 0.1 dynamic_slice.3
  17.9 5.6 %all-to-all-done = bf16[4,2,3456]{2,1,0:T(2,128)(2,1)S(1)} async-done(((bf16[4,2,3456]{2,1,0:T(2,128)(2,1)}), bf16[4,2,3456]{2,1,0:T(2,128)(2,1)S(1)}, u32[]{:S(2)}, u32[]{:S(2)}) %all-to-all-start) | async-done | bytes 55328 | tf_op jit(solution)/shard_map/all_to_all | solution.py:19
  23.6 1.4 %reshape.96 = bf16[96,1,3,2,2,2,12]{6,5,4,3,2,1,0:T(2,128)(2,1)S(1)} reshape(bf16[4,2,3456]{2,1,0:T(2,128)(2,1)S(1)} %all-to-all-done) | data formatting | bytes 110592
  25.0 1.0 %copy.32 = bf16[4,24,3,2,2,2,1,12]{1,0,5,7,4,3,2,6:T(4,128)(2,1)S(1)} copy(bf16[4,24,3,2,2,2,1,12]{7,5,4,3,2,1,0,6:T(2,128)(2,1)S(1)} %bitcast.38) | data formatting | bytes 110592 | tf_op jit(solution)/shard_map/all_to_all | solution.py:19
  26.0 0.0 copy-start.1
  26.0 0.2 copy.21
  26.2 0.2 copy.22
  26.4 7.6 %all_gather.3 = bf16[24,3,8,2,2,1,48]{6,0,5,4,3,1,2:T(8,128)(2,1)S(1)} all-gather(bf16[24,3,2,2,2,1,48]{6,0,5,4,3,1,2:T(8,128)(2,1)S(1)} %copy.22), channel_id=1, replica_groups=mesh['band'=4,'lev'=4,'grp'=2] {'lev'}, dimensions={2}, use_global_device_ids=true | all-gather | bytes 276480 | tf_op jit(solution)/shard_map/all_gather | solution.py:20
  34.0 0.2 copy_dynamic-update-slice_fusion
  34.2 0.0 copy-done.1
  34.2 0.3 fusion
  34.6 0.2 fusion.2
  34.8 0.0 copy-done
  34.8 0.4 fusion.4
  35.2 2.1 %copy.27 = f32[24,2,4,8,2,12]{0,3,4,2,1,5:T(8,128)} copy(f32[24,2,4,8,2,12]{5,3,4,2,1,0:T(8,128)S(1)} %fusion.4) | data formatting | bytes 294912 | tf_op jit(solution)/shard_map/dot_general | solution.py:38
  37.3 0.0 reduce-scatter.2.cloned.1.call-update
  37.3 0.1 broadcast_add_fusion
  37.4 15.2 %reduce-scatter.2.cloned.1.call-done = f32[24,2,4,8,2,6]{0,3,4,2,1,5:T(8,128)} async-done(((f32[24,2,4,8,2,12]{0,3,4,2,1,5:T(8,128)}), f32[24,2,4,8,2,6]{0,3,4,2,1,5:T(8,128)}) %reduce-scatter.2.cloned.1.call-update) | async-done | bytes 73744 | tf_op jit(solution)/shard_map/reduce_scatter | solution.py:41
  52.6 1.0 %select_convert_fusion = bf16[24,2,4,8,2,6]{0,3,4,2,1,5:T(8,128)(2,1)S(1)} fusion(f32[24,2,4,8,2,6]{0,3,4,2,1,5:T(8,128)} %reduce-scatter.2.cloned.1.call-done, pred[24,2,6]{0,1,2:T(4,128)(4,1)S(1)} %add_compare_fusion), kind=kLoop, calls=%fused_computation.13 | loop fusion | flops 18432 | bytes 110880 | tf_op jit(solution)/shard_map/convert_element_type | solution.py:54
  53.6 0.8 %copy.28 = bf16[24,2,4,8,2,6]{0,4,5,3,2,1:T(2,128)(2,1)} copy(bf16[24,2,4,8,2,6]{0,3,4,2,1,5:T(8,128)(2,1)S(1)} %select_convert_fusion) | data formatting | bytes 73728 | tf_op jit(solution)/shard_map/convert_element_type | solution.py:54
  (4 shorter events, 0.1 us)
Async XLA Ops:
  6.5 28.3 %copy-start = (bf16[24,2,12,1,48]{4,1,3,2,0:T(2,128)(2,1)S(1)}, bf16[24,2,12,1,48]{4,1,3,2,0:T(2,128)(2,1)}, u32[]{:S(2)}) copy-start(bf16[24,2,12,1,48]{4,1,3,2,0:T(2,128)(2,1)} %param.6) | copy-start | bytes 165892
  6.5 11.3 %copy-start.2 = (s32[96]{0:T(128)S(1)}, s32[96]{0:T(128)}, u32[]{:S(2)}) copy-start(s32[96]{0:T(128)} %param.8) | copy-start | bytes 1156
  11.5 12.1 %all-to-all-start = ((bf16[4,2,3456]{2,1,0:T(2,128)(2,1)}), bf16[4,2,3456]{2,1,0:T(2,128)(2,1)S(1)}, u32[]{:S(2)}, u32[]{:S(2)}) async-start(bf16[4,2,3456]{2,1,0:T(2,128)(2,1)} %reshape.95), calls=%async_computation | async-start | bytes 110592 | tf_op jit(solution)/shard_map/all_to_all | solution.py:19
  17.9 34.7 %reduce-scatter.2.cloned.1.call-start = ((), (), s32[]{:S(2)}) async-start(), calls=%async_computation.2 | async-start | bytes 1179648 | tf_op jit(solution)/shard_map/reduce_scatter | solution.py:41
  26.0 8.2 %copy-start.1 = (f32[8,8]{1,0:T(8,128)S(1)}, f32[8,8]{1,0:T(8,128)}, u32[]{:S(2)}) copy-start(f32[8,8]{1,0:T(8,128)} %param.9) | copy-start | bytes 772
Sparse Core Ops, SparseCore 0:
  37.4 15.1 reduce-scatter.1
where the time goes:
time: 61.6 us; the launch traced here: 61.3 us
  waiting for transfers between devices  20.9 us (34%)
  between operations  13.5 us (22%)
  local copies, waits for them, and re-layouts  8.37 us (14%)
  blocking collectives  7.56 us (12%)
  starting transfers between devices  6.35 us (10%)
  other arithmetic  3.09 us (5%)
  matrix products  1.56 us (3%)
    reduce_scatter x1, waiting for transfers between devices, body(): lax.psum_scatter(partial_value, 'grp', scatter_dimension=5, tiled=True)  15.2 us
    all_gather x1, blocking collectives, body(): coeffs = lax.all_gather(at_owners, 'lev', axis=2, tiled=True)  7.56 us
    all_to_all x1, starting transfers between devices, body(): lax.all_to_all(ordered, 'band', split_axis=0, concat_axis=6, tiled=True)  6.35 us
    all_to_all x1, waiting for transfers between devices, body(): lax.all_to_all(ordered, 'band', split_axis=0, concat_axis=6, tiled=True)  5.63 us
    unnamed x9, local copies, waits for them, and re-layouts  3.28 us
    dot_general x1, local copies, waits for them, and re-layouts, body(): lax.dot_general(parity, legendre, (((5, 6), (3, 4)), ((0, 4), (0, 1))), p...  2.07 us
    all_to_all x3, local copies, waits for them, and re-layouts, body(): lax.all_to_all(ordered, 'band', split_axis=0, concat_axis=6, tiled=True)  1.41 us
  transfers between devices with their start and end apart: 2, of which 2 were waited for; matrix products, arithmetic and copies ran while one was open for 0% of the time, Pallas kernels for 0%

commit v1 on v0

--- a/solution.py
+++ b/solution.py
@@ -38,15 +38,21 @@
     partial_value = lax.dot_general(
         parity, legendre, (((5, 6), (3, 4)), ((0, 4), (0, 1))), preferred_element_type=jnp.float32
     )
-    summed = lax.psum_scatter(partial_value, "grp", scatter_dimension=5, tiled=True)
+    groups = lax.axis_size("grp")
+    half_count = partial_value.shape[5] // groups
+    me = lax.axis_index("grp")
+    summed = lax.dynamic_slice_in_dim(partial_value, me * half_count, half_count, 5)
+    for step in range(1, groups):
+        target = lax.rem(me + step, groups)
+        piece = lax.dynamic_slice_in_dim(partial_value, target * half_count, half_count, 5)
+        summed = summed + lax.ppermute(
+            piece, "grp", [(i, (i + step) % groups) for i in range(groups)]
+        )
     slot_count = summed.shape[0]
-    half_count = summed.shape[5]
     slot_waves = lax.dynamic_slice_in_dim(
         wave_slots, lax.axis_index("band") * slot_count, slot_count
     )
-    block_start = (
-        lax.axis_index("lev") * lax.axis_size("grp") + lax.axis_index("grp")
-    ) * half_count
+    block_start = (lax.axis_index("lev") * groups + me) * half_count
     half_ids = block_start + lax.broadcasted_iota(jnp.int32, (1, 1, half_count), 2)
     parity_ids = lax.broadcasted_iota(jnp.int32, (1, 2, 1), 1)
     total = slot_waves[:, None, None] + 2 * half_ids + parity_ids

time: 61.6 us -> 44 us (0.71)
  between operations: 13.5 us -> 0.12 us
  waiting for transfers between devices: 20.9 us -> 14.6 us
  local copies, waits for them, and re-layouts: 8.37 us -> 9.87 us
  starting transfers between devices: 6.35 us -> 7.84 us
  other arithmetic: 3.09 us -> 2.1 us
    reduce_scatter x1 -> x0, waiting for transfers between devices: 15.2 us -> none  [body(): lax.psum_scatter(partial_value, 'grp', scatter_dimension=5, tiled=True)]
    ppermute x0 -> x1, waiting for transfers between devices: none -> 9.08 us  [body(): lax.ppermute(piece, 'grp', [(i, (i + step) % groups) for i in range(group...]
    dynamic_slice x0 -> x2, local copies, waits for them, and re-layouts: none -> 2.57 us  [body(): lax.dynamic_slice_in_dim(partial_value, target * half_count, half_count, 5)]
    dot_general x1 -> x0, local copies, waits for them, and re-layouts: 2.07 us -> none  [body(): lax.dot_general(parity, legendre, (((5, 6), (3, 4)), ((0, 4), (0, 1))), p...]
    ppermute x0 -> x1, starting transfers between devices: none -> 1.49 us  [body(): lax.ppermute(piece, 'grp', [(i, (i + step) % groups) for i in range(group...]
    unnamed x9 -> x10, local copies, waits for them, and re-layouts: 3.28 us -> 4.28 us
    convert_element_type x1, other arithmetic: 1.04 us -> 0.05 us  [body(): return jnp.where(valid, summed, 0.0).astype(jnp.bfloat16)]
  transfers between devices with their start and end apart: 2 -> 2, of which waited for: 2 -> 2; matrix products, arithmetic and copies ran while one was open for 0% -> 3% of each run, Pallas kernels for 0% -> 0%
where the time goes in v1:
time: 44 us; the launch traced here: 43.7 us
  waiting for transfers between devices  14.6 us (33%)
  local copies, waits for them, and re-layouts  9.87 us (22%)
  starting transfers between devices  7.84 us (18%)
  blocking collectives  7.56 us (17%)
  other arithmetic  2.1 us (5%)
  matrix products  1.56 us (4%)
    ppermute x1, waiting for transfers between devices, body(): lax.ppermute(piece, 'grp', [(i, (i + step) % groups) for i in range(group...  9.08 us
    all_gather x1, blocking collectives, body(): coeffs = lax.all_gather(at_owners, 'lev', axis=2, tiled=True)  7.56 us
    all_to_all x1, starting transfers between devices, body(): lax.all_to_all(ordered, 'band', split_axis=0, concat_axis=6, tiled=True)  6.35 us
    all_to_all x1, waiting for transfers between devices, body(): lax.all_to_all(ordered, 'band', split_axis=0, concat_axis=6, tiled=True)  5.56 us
    unnamed x10, local copies, waits for them, and re-layouts  4.28 us
    dynamic_slice x2, local copies, waits for them, and re-layouts, body(): lax.dynamic_slice_in_dim(partial_value, target * half_count, half_count, 5)  2.57 us
    ppermute x1, starting transfers between devices, body(): lax.ppermute(piece, 'grp', [(i, (i + step) % groups) for i in range(group...  1.49 us
    all_to_all x3, local copies, waits for them, and re-layouts, body(): lax.all_to_all(ordered, 'band', split_axis=0, concat_axis=6, tiled=True)  1.41 us
  transfers between devices with their start and end apart: 2, of which 2 were waited for; matrix products, arithmetic and copies ran while one was open for 3% of the time, Pallas kernels for 0%

profile of v1, /device:TPU:0, one launch (start us, length us, event | category | flops | bytes accessed | tf_op | source)
XLA Modules:
  0.0 43.7 jit_solution(1349688747209076095)
XLA Ops:
  0.0 0.0 copy-start
  0.0 0.0 copy-start.2
  0.0 0.7 %minimum_bitcast_fusion = s32[12]{0:T(128)S(1)} fusion(s32[1,12]{1,0:T(1,128)} %param.7), kind=kLoop, calls=%fused_computation.34 | loop fusion | flops 204 | bytes 96 | tf_op jit(solution)/shard_map/le | solution.py:11
  0.7 0.1 iota_compare_fusion.1
  0.8 1.0 %fusion.9 = bf16[3,2,2,2,12,96]{5,3,4,2,1,0:T(2,128)(2,1)S(1)} fusion(bf16[3,2,2,2,1,12,96]{6,3,5,4,2,1,0:T(2,128)(2,1)} %param.5, pred[12,96]{1,0:T(8,128)(4,1)S(1)} %iota_compare_fusion.1), kind=kLoop, calls=%fused_computation.19 | loop fusion | flops 27648 | bytes 111744 | tf_op jit(solution)/shard_map/reshape.5
  1.8 0.9 %fusion.1 = bf16[96,3,2,2,2,1,12]{0,6,4,3,2,1,5:T(8,128)(2,1)S(1)} fusion(bf16[3,2,2,2,12,96]{5,3,4,2,1,0:T(2,128)(2,1)S(1)} %fusion.9, s32[96]{0:T(128)} %param.8), kind=kOutput, calls=%fused_computation.3 | convolution fusion | flops 5345280 | bytes 110976 | tf_op jit(solution)/shard_map/dot_general | solution.py:16
  2.7 0.7 %copy.31 = bf16[96,3,2,2,2,1,12]{6,4,3,2,1,5,0:T(2,128)(2,1)S(1)} copy(bf16[96,3,2,2,2,1,12]{0,6,4,3,2,1,5:T(8,128)(2,1)S(1)} %fusion.1) | data formatting | bytes 110592 | tf_op jit(solution)/shard_map/convert_element_type | solution.py:18
  3.3 1.7 %reshape.95 = bf16[4,2,3456]{2,1,0:T(2,128)(2,1)} reshape(bf16[96,1,3,2,2,2,12]{6,5,4,3,2,1,0:T(2,128)(2,1)S(1)} %bitcast.37) | data formatting | bytes 110592
  5.0 6.3 %all-to-all-start = ((bf16[4,2,3456]{2,1,0:T(2,128)(2,1)}), bf16[4,2,3456]{2,1,0:T(2,128)(2,1)S(1)}, u32[]{:S(2)}, u32[]{:S(2)}) async-start(bf16[4,2,3456]{2,1,0:T(2,128)(2,1)} %reshape.95), calls=%async_computation | async-start | bytes 110592 | tf_op jit(solution)/shard_map/all_to_all | solution.py:19
  11.3 0.0 copy-done.2
  11.3 0.1 dynamic_slice.9
  11.4 0.1 broadcast_add_fusion
  11.5 5.6 %all-to-all-done = bf16[4,2,3456]{2,1,0:T(2,128)(2,1)S(1)} async-done(((bf16[4,2,3456]{2,1,0:T(2,128)(2,1)}), bf16[4,2,3456]{2,1,0:T(2,128)(2,1)S(1)}, u32[]{:S(2)}, u32[]{:S(2)}) %all-to-all-start) | async-done | bytes 55328 | tf_op jit(solution)/shard_map/all_to_all | solution.py:19
  17.0 1.4 %reshape.96 = bf16[96,1,3,2,2,2,12]{6,5,4,3,2,1,0:T(2,128)(2,1)S(1)} reshape(bf16[4,2,3456]{2,1,0:T(2,128)(2,1)S(1)} %all-to-all-done) | data formatting | bytes 110592
  18.4 1.0 %copy.45 = bf16[4,24,3,2,2,2,1,12]{1,0,5,7,4,3,2,6:T(4,128)(2,1)S(1)} copy(bf16[4,24,3,2,2,2,1,12]{7,5,4,3,2,1,0,6:T(2,128)(2,1)S(1)} %bitcast.38) | data formatting | bytes 110592 | tf_op jit(solution)/shard_map/all_to_all | solution.py:19
  19.5 0.0 copy-start.1
  19.5 0.2 copy.33
  19.7 0.2 copy.34
  19.9 7.6 %all_gather.3 = bf16[24,3,8,2,2,1,48]{6,0,5,4,3,1,2:T(8,128)(2,1)S(1)} all-gather(bf16[24,3,2,2,2,1,48]{6,0,5,4,3,1,2:T(8,128)(2,1)S(1)} %copy.34), channel_id=1, replica_groups=mesh['band'=4,'lev'=4,'grp'=2] {'lev'}, dimensions={2}, use_global_device_ids=true | all-gather | bytes 276480 | tf_op jit(solution)/shard_map/all_gather | solution.py:20
  27.4 0.2 copy_dynamic-update-slice_fusion
  27.7 0.0 copy-done.1
  27.7 0.3 fusion
  28.0 0.2 fusion.2
  28.3 0.0 copy-done
  28.3 0.4 fusion.4
  28.7 0.9 %constant_dynamic-slice_fusion = (f32[24,2,4,8,2,6]{5,3,4,2,1,0:T(8,128)S(1)}, f32[24,2,4,8,2,6]{5,3,4,2,1,0:T(8,128)S(1)}) fusion(f32[24,2,4,8,2,12]{5,3,4,2,1,0:T(8,128)S(1)} %fusion.4, s32[]{:T(128)S(6)} %select_n.31, s32[]{:T(128)S(6)} %select_n.30), kind=kLoop, calls=%fused_computation.36 | loop fusion | bytes 294920 | tf_op jit(solution)/shard_map/dynamic_slice | solution.py:47
  29.5 1.7 %copy.40 = f32[24,2,4,8,2,6]{0,3,5,4,2,1:T(8,128)} copy(f32[24,2,4,8,2,6]{5,3,4,2,1,0:T(8,128)S(1)} %get-tuple-element.5) | data formatting | bytes 147456 | tf_op jit(solution)/shard_map/dynamic_slice | solution.py:47
  31.2 1.5 %collective-permute-start = (f32[24,2,4,8,2,6]{0,3,5,4,2,1:T(8,128)}, f32[24,2,4,8,2,6]{0,3,5,4,2,1:T(8,128)S(1)}, u32[]{:S(2)}, u32[]{:S(2)}) collective-permute-start(f32[24,2,4,8,2,6]{0,3,5,4,2,1:T(8,128)} %copy.40), channel_id=1, source_target_pairs={{0,1},{1,0},{2,3},{3,2},{4,5},{5,4},{6,7},{7,6},{8,9},{9,8},{10,11... | collective-permute-start | bytes 221192 | tf_op jit(solution)/shard_map/ppermute | solution.py:48
  32.7 1.0 %copy.49 = f32[24,2,4,8,2,6]{0,3,5,4,2,1:T(8,128)S(1)} copy(f32[24,2,4,8,2,6]{5,3,4,2,1,0:T(8,128)S(1)} %get-tuple-element.6) | data formatting | bytes 147456
  33.7 9.1 %collective-permute-done = f32[24,2,4,8,2,6]{0,3,5,4,2,1:T(8,128)S(1)} collective-permute-done((f32[24,2,4,8,2,6]{0,3,5,4,2,1:T(8,128)}, f32[24,2,4,8,2,6]{0,3,5,4,2,1:T(8,128)S(1)}, u32[]{:S(2)}, u32[]{:S(2)}) %collective-permute-start) | collective-permute-done | bytes 73760 | tf_op jit(solution)/shard_map/ppermute | solution.py:48
  42.8 0.1 select_convert_fusion
  42.9 0.8 %copy.41 = bf16[24,2,4,8,2,6]{0,4,5,3,2,1:T(2,128)(2,1)} copy(bf16[24,2,4,8,2,6]{0,3,5,4,2,1:T(8,128)(2,1)S(1)} %select_convert_fusion) | data formatting | bytes 73728 | tf_op jit(solution)/shard_map/convert_element_type | solution.py:60
  (4 shorter events, 0.1 us)
Async XLA Ops:
  0.0 28.3 %copy-start = (bf16[24,2,12,1,48]{4,1,3,2,0:T(2,128)(2,1)S(1)}, bf16[24,2,12,1,48]{4,1,3,2,0:T(2,128)(2,1)}, u32[]{:S(2)}) copy-start(bf16[24,2,12,1,48]{4,1,3,2,0:T(2,128)(2,1)} %param.6) | copy-start | bytes 165892
  0.0 11.3 %copy-start.2 = (s32[96]{0:T(128)S(1)}, s32[96]{0:T(128)}, u32[]{:S(2)}) copy-start(s32[96]{0:T(128)} %param.8) | copy-start | bytes 1156
  5.0 12.1 %all-to-all-start = ((bf16[4,2,3456]{2,1,0:T(2,128)(2,1)}), bf16[4,2,3456]{2,1,0:T(2,128)(2,1)S(1)}, u32[]{:S(2)}, u32[]{:S(2)}) async-start(bf16[4,2,3456]{2,1,0:T(2,128)(2,1)} %reshape.95), calls=%async_computation | async-start | bytes 110592 | tf_op jit(solution)/shard_map/all_to_all | solution.py:19
  19.5 8.2 %copy-start.1 = (f32[8,8]{1,0:T(8,128)S(1)}, f32[8,8]{1,0:T(8,128)}, u32[]{:S(2)}) copy-start(f32[8,8]{1,0:T(8,128)} %param.9) | copy-start | bytes 772
  31.2 11.6 %collective-permute-start = (f32[24,2,4,8,2,6]{0,3,5,4,2,1:T(8,128)}, f32[24,2,4,8,2,6]{0,3,5,4,2,1:T(8,128)S(1)}, u32[]{:S(2)}, u32[]{:S(2)}) collective-permute-start(f32[24,2,4,8,2,6]{0,3,5,4,2,1:T(8,128)} %copy.40), channel_id=1, source_target_pairs={{0,1},{1,0},{2,3},{3,2},{4,5},{5,4},{6,7},{7,6},{8,9},{9,8},{10,11... | collective-permute-start | bytes 221192 | tf_op jit(solution)/shard_map/ppermute | solution.py:48
